TPU v7x, 256 devices: a whole 4x4x8 slice. The times are simulated.
256 devices in a mesh: chan: 32 (over x_lo, z, core), stn: 8 (over x_hi, y).
Axes of the slice: x: 4 (x_hi: 2, x_lo: 2; x = x_hi * 2 + x_lo), y: 4, z: 8, core: 2. Of those that a mesh axis runs over, the one named last changes fastest.
Arguments:
- voltages: bfloat16 [32, 2, 1024, 512], P(None, None, ('stn', 'chan')), may hold values from -6 to 6
- phase_index: int32 [1024], P(('stn', 'chan')), may hold values from 0 to 1023
- int_lengths: int32 [4], replicated, may hold values from 1 to 192, 512 in all
- beam_weights: bfloat16 [2, 256, 1024], replicated, may hold values from -0.1875 to 0.1875
Outputs:
- visibilities: bfloat16 [8, 5, 4, 32, 2, 128, 128], P('stn', None, None, 'chan')
- beam_power: float32 [4, 32, 256], P(None, 'chan', 'stn')
Inputs may be any that keep to these rules, and one draw needn't show every extreme that they name: `int_lengths`: 4 integration lengths summing to 512; the longest is exactly 192.
All inputs are finite; a program needn't handle non-finite values.
Results may differ from a plain program's by a relative error of at most 0.0055.
Values may be sent and summed in bfloat16 or wider, within the bound.
A program may use at most 64 MiB of HBM per device.

v0:
```python
import math

import jax
import jax.numpy as jnp
from jax import lax
from jax.sharding import PartitionSpec as P

INTEG = 4
MOST = 192
BEAMS = 256
PHASES = 1024


full_turn = 2.0 * math.pi


def rotate(voltages, phase_index, channel):
    phase_turns = channel[:, None] * phase_index[None, :] % PHASES
    phase_angle = phase_turns.astype(jnp.float32) * (full_turn / PHASES)
    cosine = jnp.cos(phase_angle)[:, :, None]
    sine_part = jnp.sin(phase_angle)[:, :, None]
    real_in = voltages[:, 0].astype(jnp.float32)
    imag_in = voltages[:, 1].astype(jnp.float32)
    return jnp.stack(
        [real_in * cosine + imag_in * sine_part, imag_in * cosine - real_in * sine_part], axis=1
    ).astype(jnp.bfloat16)


def windows(block, starts, int_lengths):
    padded = jnp.pad(block, ((0, 0), (0, 0), (0, MOST)))
    in_range = jnp.arange(MOST, dtype=jnp.int32)
    result = []
    for period in range(INTEG):
        segment = lax.dynamic_slice_in_dim(padded, starts[period], MOST, 2)
        keep_mask = (in_range < int_lengths[period])[None, None, :]
        result.append(jnp.where(keep_mask, segment, jnp.zeros_like(segment)))
    return jnp.stack(result)


def correlate(own_parts, other, starts, int_lengths):
    padded = jnp.pad(other, ((0, 0), (0, 0), (0, MOST)))
    block_rows = own_parts.shape[2] // 2
    result = []
    for period in range(INTEG):
        segment = lax.dynamic_slice_in_dim(padded, starts[period], MOST, 2)
        products = jnp.einsum(
            "cal,cbl->cab", own_parts[period], segment, preferred_element_type=jnp.float32
        )
        real_part = products[:, :block_rows, :block_rows] + products[:, block_rows:, block_rows:]
        imag_part = products[:, block_rows:, :block_rows] - products[:, :block_rows, block_rows:]
        inverse = 1.0 / int_lengths[period].astype(jnp.float32)
        result.append((jnp.stack([real_part, imag_part], axis=1) * inverse).astype(jnp.bfloat16))
    return jnp.stack(result)


def stack_weights(beam_weights, beam_first, beam_count, column_first, column_count):
    weight_real = lax.dynamic_slice(
        beam_weights[0], (beam_first, column_first), (beam_count, column_count)
    )
    weight_imag = lax.dynamic_slice(
        beam_weights[1], (beam_first, column_first), (beam_count, column_count)
    )
    upper = jnp.concatenate([weight_real, -weight_imag], axis=1)
    lower = jnp.concatenate([weight_imag, weight_real], axis=1)
    return jnp.concatenate([upper, lower], axis=0)


def integrate(power, starts, int_lengths, form):
    samples = power.shape[-1]
    sample_index = jnp.arange(samples, dtype=jnp.int32)[None, :]
    in_window = (
        (sample_index >= starts[:, None]) & (sample_index < (starts + int_lengths)[:, None])
    ).astype(jnp.float32)
    summed = jnp.einsum(form, power, in_window, precision=lax.Precision.HIGHEST)
    return summed / int_lengths.astype(jnp.float32)[:, None, None]


def local(voltages, phase_index, int_lengths, beam_weights):
    channel = jnp.arange(voltages.shape[0], dtype=jnp.int32)
    rotated = rotate(voltages, phase_index, channel)
    turned = lax.all_to_all(rotated, "chan", split_axis=0, concat_axis=2, tiled=True)
    station = lax.axis_index("stn")
    stations = lax.axis_size("stn")
    halfway = stations // 2
    share = BEAMS // stations
    ch_local, _, block_rows, samples = turned.shape
    own = turned.reshape(ch_local, 2 * block_rows, samples)
    starts = jnp.cumsum(int_lengths) - int_lengths
    own_parts = windows(own, starts, int_lengths)

    def place(vis_total, other, offset):
        fresh = correlate(own_parts, other, starts, int_lengths)
        return lax.dynamic_update_slice(vis_total, fresh[None], (offset, 0, 0, 0, 0, 0))

    def leave(vis_total, other, offset):
        return vis_total

    vis_start = jnp.zeros((halfway + 1, INTEG, ch_local, 2, block_rows, block_rows), jnp.bfloat16)
    beam_start = jnp.zeros((ch_local, 2 * share, samples), jnp.float32)
    portion = lax.all_gather(turned, "stn", axis=2, tiled=True)
    first_row = jnp.int32(0)
    vis_total = vis_start
    beam_total = beam_start
    for member in range(portion.shape[2] // block_rows):
        other = portion[:, :, member * block_rows : (member + 1) * block_rows, :].reshape(
            ch_local, 2 * block_rows, samples
        )
        other_index = first_row // block_rows + member
        offset = (other_index - station) % stations
        vis_total = lax.cond(offset <= halfway, place, leave, vis_total, other, offset)
        stacked = stack_weights(
            beam_weights, station * share, share, other_index * block_rows, block_rows
        )
        partial_beam = jnp.einsum("rk,ckt->crt", stacked, other, preferred_element_type=jnp.float32)
        beam_total = beam_total + lax.optimization_barrier(
            partial_beam.astype(jnp.bfloat16)
        ).astype(jnp.float32)
    vis_total, beam_total = (vis_total, beam_total)
    beam_total = beam_total.reshape(ch_local, 2, share, samples)
    power = beam_total[:, 0] ** 2 + beam_total[:, 1] ** 2
    beam_power = integrate(power, starts, int_lengths, "cbt,jt->jcb")
    return (vis_total[None], beam_power)


def solution(mesh):
    return jax.shard_map(
        local,
        mesh=mesh,
        in_specs=(P(None, None, ("stn", "chan"), None), P(("stn", "chan")), P(), P()),
        out_specs=(P("stn", None, None, "chan", None, None, None), P(None, "chan", "stn")),
        check_vma=False,
    )
```

profile of v0, /device:TPU:1, one launch (start us, length us, event | category | flops | bytes accessed | tf_op | source)
XLA Modules:
  0.0 167.8 jit_solution(5252909715909642435)
XLA Ops:
  7.2 0.8 fusion.347
  8.2 1.2 fusion.273
  9.6 22.5 %all_to_all.18 = bf16[32,2,4,512]{3,2,1,0:T(4,128)(2,1)S(1)} all-to-all(bf16[32,2,4,512]{3,2,1,0:T(4,128)(2,1)S(1)} %pad_maximum_fusion), channel_id=1, replica_groups=mesh['chan'=32,'stn'=8] {'chan'}, dimensions={0} | all-to-all | bytes 524288 | tf_op jit(solution)/shard_map/all_to_all | solution.py:81
  32.2 0.8 all_to_all.16
  33.2 0.6 fusion.384
  40.9 0.6 fusion.383
  41.5 1.2 iota_compare_fusion.3
  42.7 1.1 iota_compare_fusion.5
  44.0 0.3 fusion.279
  44.3 44.1 %all-gather.2.cloned.1.call-done = bf16[1,2,1024,512]{3,2,1,0:T(8,128)(2,1)} async-done(((bf16[1,2,128,512]{3,2,1,0:T(8,128)(2,1)}), bf16[1,2,1024,512]{3,2,1,0:T(8,128)(2,1)}) %all-gather.2.cloned.1.call-update) | async-done | bytes 2097168 | tf_op jit(solution)/shard_map/all_gather | solution.py:100
  88.4 1.7 %fusion.380 = (bf16[1,2,128,512]{3,2,1,0:T(8,128)(2,1)S(1)}, bf16[1,2,128,512]{3,2,1,0:T(8,128)(2,1)S(1)}, bf16[1,2,128,512]{3,2,1,0:T(8,128)(2,1)S(1)}, bf16[1,...) fusion(bf16[1,2,1024,512]{3,2,1,0:T(8,128)(2,1)} %all-gather.2., ...), kind=kLoop, calls=%fused_computation.561 | loop fusion | bytes 4194304 | tf_op jit(solution)/shard_map/slice | solution.py:105
  91.4 13.8 %conditional.8 = (bf16[5,4,1,2,128,128]{4,5,3,1,2,0:T(8,128)(2,1)}) conditional(s32[]{:T(128)} %convert_element_type.674, () %tuple.58, (bf16[1,2,128,512]{3,2,1,0:T(8,128)(2,1)S(1)}, s32[4]{0:T(128)S(1)}, bf16[1,256,192]{2,1,0:T(8,128)(2,1)S(1)}, s32[4]{0:T(128)S(1)}, bf16[1,256,192]{2,1,0:T(8,128)(2,1)S(1)}, ...), branch_computations={%region_1.2_spmd, %region_2.3_spmd} | conditional | flops 102236168 | bytes 6685032 | solution.py:110
  91.5 0.7 fusion.364
  93.8 0.2 convolution_bitcast_fusion.2
  96.6 0.2 convolution_bitcast_fusion.1
  99.3 0.2 convolution_bitcast_fusion
  102.2 0.2 convolution_bitcast_fusion.3
  103.1 1.4 broadcast_in_dim.57
  104.5 0.7 fusion
  105.2 13.0 %conditional.9 = (bf16[5,4,1,2,128,128]{4,5,3,1,2,0:T(8,128)(2,1)}) conditional(s32[]{:T(128)} %convert_element_type.673, bf16[5,4,1,2,128,128]{4,5,3,1,2,0:T(8,128)(2,1)} %get-tuple-element.511, (bf16[1,2,128,512]{3,2,1,0:T(8,128)(2,1)S(1)}, s32[4]{0:T(128)S(1)}, bf16[1,256,192]{2,1,0:T(8,128)(2,1)S(1)}, s32[4]{0:T(128)S(1)}, ...), branch_computations={%region_3.4_spmd, %region_4.5_spmd} | conditional | flops 102236168 | bytes 5374310 | solution.py:110
  105.2 0.7 fusion.366
  108.0 0.2 convolution_bitcast_fusion.7
  110.9 0.2 convolution_bitcast_fusion.6
  113.7 0.2 convolution_bitcast_fusion.5
  116.5 0.2 convolution_bitcast_fusion.4
  117.5 0.7 fusion.33
  118.2 13.0 %conditional.10 = (bf16[5,4,1,2,128,128]{4,5,3,1,2,0:T(8,128)(2,1)}) conditional(s32[]{:T(128)} %convert_element_type.672, bf16[5,4,1,2,128,128]{4,5,3,1,2,0:T(8,128)(2,1)} %get-tuple-element.512, (bf16[1,2,128,512]{3,2,1,0:T(8,128)(2,1)S(1)}, s32[4]{0:T(128)S(1)}, bf16[1,256,192]{2,1,0:T(8,128)(2,1)S(1)}, s32[4]{0:T(128)S(1)}, ...), branch_computations={%region_5.6_spmd, %region_6.7_spmd} | conditional | flops 102236168 | bytes 5374310 | solution.py:110
  118.2 0.7 fusion.368
  121.0 0.2 convolution_bitcast_fusion.11
  124.0 0.2 convolution_bitcast_fusion.10
  126.8 0.2 convolution_bitcast_fusion.9
  129.6 0.2 convolution_bitcast_fusion.8
  130.5 0.7 fusion.66
  131.2 13.0 %conditional.11 = (bf16[5,4,1,2,128,128]{4,5,3,1,2,0:T(8,128)(2,1)}) conditional(s32[]{:T(128)} %convert_element_type.671, bf16[5,4,1,2,128,128]{4,5,3,1,2,0:T(8,128)(2,1)} %get-tuple-element.513, (bf16[1,2,128,512]{3,2,1,0:T(8,128)(2,1)S(1)}, s32[4]{0:T(128)S(1)}, bf16[1,256,192]{2,1,0:T(8,128)(2,1)S(1)}, s32[4]{0:T(128)S(1)}, ...), branch_computations={%region_7.8_spmd, %region_8.9_spmd} | conditional | flops 102236168 | bytes 5374310 | solution.py:110
  131.2 0.7 fusion.370
  134.0 0.2 convolution_bitcast_fusion.15
  137.0 0.2 convolution_bitcast_fusion.14
  139.8 0.2 convolution_bitcast_fusion.13
  143.5 0.7 fusion.99
  144.2 13.0 %conditional.12 = (bf16[5,4,1,2,128,128]{4,5,3,1,2,0:T(8,128)(2,1)}) conditional(s32[]{:T(128)} %convert_element_type.670, bf16[5,4,1,2,128,128]{4,5,3,1,2,0:T(8,128)(2,1)} %get-tuple-element.514, (bf16[1,2,128,512]{3,2,1,0:T(8,128)(2,1)S(1)}, s32[4]{0:T(128)S(1)}, bf16[1,256,192]{2,1,0:T(8,128)(2,1)S(1)}, s32[4]{0:T(128)S(1)}, ...), branch_computations={%region_9.10_spmd, %region_10.11_spmd} | conditional | flops 102236168 | bytes 5374310 | solution.py:110
  144.2 0.7 fusion.372
  152.8 0.2 convolution_bitcast_fusion.17
  155.6 0.2 convolution_bitcast_fusion.16
  156.5 0.7 fusion.132
  157.3 0.8 convolution_divide_fusion
  158.1 1.8 %conditional.15 = (bf16[1,5,4,1,2,128,128]{6,5,4,3,2,1,0:T(8,128)(2,1)S(1)}) conditional(s32[]{:T(128)} %convert_element_type.667, bf16[5,4,1,2,128,128]{4,5,3,1,0,2:T(8,128)(2,1)} %bitcast.320, (bf16[5,4,1,2,128,128]{4,5,3,1,2,0:T(8,128)(2,1)}, bf16[1,2,128,512]{3,2,1,0:T(8,128)(2,1)S(1)}, s32[4]{0:T(128)S(1)}, ...), branch_computations={%region_15.16_spmd, %region_16.17_spmd} | conditional | flops 102236168 | bytes 7995750 | solution.py:110
  158.1 1.8 %copy.20 = bf16[1,5,4,1,2,128,128]{6,5,4,3,2,1,0:T(8,128)(2,1)S(1)} copy(bf16[1,5,4,1,2,128,128]{5,6,4,2,3,1,0:T(8,128)(2,1)} %bitcast.266) | data formatting | bytes 2621440 | tf_op jit(solution)/shard_map/cond
  159.9 1.0 copy-done
  (71 shorter events, 3.6 us)
Async XLA Ops:
  7.2 81.2 %all-gather.2.cloned.1.call-start = ((), (), s32[]{:S(2)}) async-start(), calls=%async_computation.1 | async-start | bytes 2359296 | tf_op jit(solution)/shard_map/all_gather | solution.py:100
  9.4 23.6 %copy-start.2 = (s32[4]{0:T(128)S(1)}, s32[4]{0:T(128)}, u32[]{:S(2)}) copy-start(s32[4]{0:T(128)} %param.22) | copy-start | bytes 52
  9.4 34.4 %copy-start.1 = (bf16[2,256,1024]{2,1,0:T(8,128)(2,1)S(1)}, bf16[2,256,1024]{2,1,0:T(8,128)(2,1)}, u32[]{:S(2)}) copy-start(bf16[2,256,1024]{2,1,0:T(8,128)(2,1)} %param.23) | copy-start | bytes 3145732
  159.9 1.1 copy-start
Sparse Core Ops, SparseCore 0:
  33.1 55.2 all-gather.1
where the time goes:
time: 169 us; the launch traced here: 168 us
  loops' own time  52 us (31%)
  waiting for transfers between devices  44.1 us (26%)
  blocking collectives  22.5 us (13%)
  between operations  21.3 us (13%)
  local copies, waits for them, and re-layouts  11.7 us (7%)
  other arithmetic  9.31 us (6%)
  matrix products  6.89 us (4%)
    another operation x8, loops' own time, local(): lax.cond(offset <= halfway, place, leave, vis_total, other, offset)  52 us
    all_gather x1, waiting for transfers between devices, local(): portion = lax.all_gather(turned, 'stn', axis=2, tiled=True)  44.1 us
    all_to_all x1, blocking collectives, local(): lax.all_to_all(rotated, 'chan', split_axis=0, concat_axis=2, tiled=True)  22.5 us
    dot_general x20, matrix products, correlate(): jnp.einsum('cal,cbl->cab', own_parts[period], segment, preferred_element_...  4.83 us
    dynamic_update_slice x5, other arithmetic, place(): lax.dynamic_update_slice(vis_total, fresh[None], (offset, 0, 0, 0, 0, 0))  3.64 us
    slice x5, local copies, waits for them, and re-layouts, correlate(): inverse = 1.0 / int_lengths[period].astype(jnp.float32)  3.38 us
  transfers between devices with their start and end apart: 1, of which 1 were waited for; matrix products, arithmetic and copies ran while one was open for 3% of the time, Pallas kernels for 0%

commit v1 on v0

v1 whole, which is shorter than its diff:
```python
import functools
import math

import jax
import jax.numpy as jnp
from jax import lax
from jax.experimental import pallas as pl
from jax.experimental.pallas import tpu as pltpu
from jax.sharding import PartitionSpec as P

INTEG = 4
BEAMS = 256
PHASES = 1024
NC = 32
NS = 8
LT = 4
SAMPLES = 512
BLK = 128
OFFS = 5
SHARE = BEAMS // NS
NCH = 2
W = LT // NCH
BF = jnp.bfloat16
F32 = jnp.float32
MESH = pl.DeviceIdType.MESH


def rotate_all(ph, vin, sbuf, trig):
    row = lax.broadcasted_iota(jnp.int32, (NC, 8, 128), 1)
    chan = lax.broadcasted_iota(jnp.int32, (NC, 8, 128), 0)
    col = row % 4
    step = jnp.where(col == 0, ph[0], jnp.where(col == 1, ph[1], jnp.where(col == 2, ph[2], ph[3])))
    turns = chan * step - jnp.where(row >= 4, PHASES // 4, 0)
    turns = ((turns + PHASES // 2) & (PHASES - 1)) - PHASES // 2
    trig[...] = jnp.cos(turns.astype(F32) * (2.0 * math.pi / PHASES))

    def one(c, carry):
        cs = trig[c]
        cos, sin = cs[0:4], cs[4:8]
        re = vin[c, 0].astype(F32)
        im = vin[c, 1].astype(F32)
        for t in range(LT):
            a = re[:, t * 128 : (t + 1) * 128]
            b = im[:, t * 128 : (t + 1) * 128]
            sbuf[c, 0, t] = (a * cos + b * sin).astype(BF)
            sbuf[c, 1, t] = (b * cos - a * sin).astype(BF)
        return carry

    lax.fori_loop(0, NC, one, 0, unroll=4)


def comm_kernel(ph, v_hbm, g, vin, sbuf, trig, lsem, s1, r1, s2, r2):
    c = lax.axis_index("chan")
    s = lax.axis_index("stn")
    barrier = pltpu.get_barrier_semaphore()

    def hello(k, carry):
        pl.semaphore_signal(
            barrier, 1, device_id={"chan": (c + k) % NC, "stn": s}, device_id_type=MESH
        )
        return carry

    lax.fori_loop(1, NC, hello, 0)
    for k in range(1, NS):
        pl.semaphore_signal(
            barrier, 1, device_id={"chan": c, "stn": (s + k) % NS}, device_id_type=MESH
        )
    load = pltpu.make_async_copy(v_hbm, vin, lsem.at[0])
    load.start()
    load.wait()
    rotate_all(ph, vin, sbuf, trig)
    pl.semaphore_wait(barrier, NC - 1 + NS - 1)

    for q in range(NCH):
        ts = pl.ds(q * W, W)

        def send(k, carry):
            d = (c + k) % NC
            pltpu.make_async_remote_copy(
                sbuf.at[d, :, ts], g.at[0, :, ts, c], s1.at[q], r1.at[q],
                device_id={"chan": d, "stn": s}, device_id_type=MESH,
            ).start()
            return carry

        lax.fori_loop(1, NC, send, 0)
    for q in range(NCH):
        ts = pl.ds(q * W, W)
        own = pltpu.make_async_copy(sbuf.at[c, :, ts], g.at[0, :, ts, c], lsem.at[1])
        own.start()
        own.wait()
    sends = []
    for q in range(NCH):
        ts = pl.ds(q * W, W)
        many = pltpu.make_async_remote_copy(
            sbuf.at[pl.ds(0, NC - 1), :, ts], g.at[0, :, ts, pl.ds(0, NC - 1)], s1.at[q], r1.at[q],
            device_id={"chan": c, "stn": (s + 1) % NS}, device_id_type=MESH,
        )
        many.wait_recv()
        for k in range(1, NS):
            cp = pltpu.make_async_remote_copy(
                g.at[0, :, ts], g.at[k, :, ts], s2.at[k - 1, q], r2.at[k - 1, q],
                device_id={"chan": c, "stn": (s - k + NS) % NS}, device_id_type=MESH,
            )
            cp.start()
            sends.append(cp)
        many.wait_send()
    for cp in sends:
        cp.wait()


def comm(phase_index, voltages):
    return pl.pallas_call(
        comm_kernel,
        out_shape=jax.ShapeDtypeStruct((NS, 2, LT, NC, 4, 128), BF),
        in_specs=[pl.BlockSpec(memory_space=pltpu.SMEM), pl.BlockSpec(memory_space=pl.ANY)],
        out_specs=pl.BlockSpec(memory_space=pltpu.VMEM),
        scratch_shapes=[
            pltpu.VMEM((NC, 2, 4, SAMPLES), BF),
            pltpu.VMEM((NC, 2, LT, 4, 128), BF),
            pltpu.VMEM((NC, 8, 128), F32),
            pltpu.SemaphoreType.DMA((2,)),
            pltpu.SemaphoreType.DMA((NCH,)),
            pltpu.SemaphoreType.DMA((NCH,)),
            pltpu.SemaphoreType.DMA((NS - 1, NCH)),
            pltpu.SemaphoreType.DMA((NS - 1, NCH)),
        ],
        compiler_params=pltpu.CompilerParams(collective_id=0, has_side_effects=True),
        name="comm",
    )(phase_index, voltages)


def window_edges(lens):
    edges = [jnp.int32(0)]
    for j in range(INTEG):
        edges.append(edges[-1] + lens[j])
    return edges


def build_windows(blk, lens, left):
    edges = window_edges(lens)
    lane = lax.broadcasted_iota(jnp.int32, (1, 128), 1)
    for t in range(LT):
        at = lane + t * 128
        for j in range(INTEG):
            keep = ((at >= edges[j]) & (at < edges[j + 1])).astype(F32).astype(BF)
            for p in range(2):
                left[j * BLK : (j + 1) * BLK, (p * LT + t) * 128 : (p * LT + t + 1) * 128] = (
                    blk[p, t] * keep
                )


def correlate(blk, lens, left, put):
    re = [blk[0, t] for t in range(LT)]
    im = [blk[1, t] for t in range(LT)]
    neg = [-x for x in im]
    right = jnp.concatenate(
        [jnp.concatenate(re + im, axis=1), jnp.concatenate(neg + re, axis=1)], axis=0
    )
    prod = lax.dot_general(
        left[...], right, (((1,), (1,)), ((), ())), preferred_element_type=F32
    )
    for j in range(INTEG):
        inverse = 1.0 / jnp.full((1, 128), lens[j], jnp.int32).astype(F32)
        for p in range(2):
            put(j, p, (prod[j * BLK : (j + 1) * BLK, p * 128 : (p + 1) * 128] * inverse).astype(BF))


def beam_part(blk, wts, q):
    cols = pl.ds(pl.multiple_of(q * BLK, BLK), BLK)
    wr = wts[0, :, cols]
    wi = wts[1, :, cols]
    stack = jnp.concatenate(
        [jnp.concatenate([wr, -wi], axis=1), jnp.concatenate([wi, wr], axis=1)], axis=0
    )
    parts = []
    for t in range(0, LT, 2):
        x = jnp.concatenate(
            [jnp.concatenate([blk[p, t], blk[p, t + 1]], axis=1) for p in range(2)], axis=0
        )
        parts.append(jnp.dot(stack, x, preferred_element_type=F32))
    return jnp.concatenate(parts, axis=1)


def beam_finish(beam, lens, out):
    power = beam[:SHARE] ** 2 + beam[SHARE:] ** 2
    edges = window_edges(lens)
    at = lax.broadcasted_iota(jnp.int32, (8, SAMPLES), 1)
    row = lax.broadcasted_iota(jnp.int32, (8, SAMPLES), 0)
    mask = jnp.zeros((8, SAMPLES), F32)
    for j in range(INTEG):
        inside = (row == j) & (at >= edges[j]) & (at < edges[j + 1])
        mask = jnp.where(inside, 1.0, mask)
    total = lax.dot_general(
        mask, power, (((1,), (1,)), ((), ())), precision=lax.Precision.HIGHEST,
        preferred_element_type=F32,
    )
    for j in range(INTEG):
        out[j] = total[j : j + 1] / jnp.full((1, SHARE), lens[j], jnp.int32).astype(F32)


def math_kernel(lens, w_hbm, g_all, vis, power, wts, left, stage, wsem, osem):
    s = lax.axis_index("stn")
    load = pltpu.make_async_copy(
        w_hbm.at[:, pl.ds(pl.multiple_of(s * SHARE, SHARE), SHARE)], wts, wsem
    )
    load.start()
    g = g_all.reshape(NS, 2, LT, BLK, 128)
    build_windows(g.at[0], lens, left)
    for k in range(OFFS):

        def put(j, p, value):
            stage[k, j, p] = value

        correlate(g.at[k], lens, left, put)
        pltpu.make_async_copy(stage.at[k], vis.at[0, k, :, 0], osem.at[k]).start()
    load.wait()
    beam = jnp.zeros((2 * SHARE, SAMPLES), F32)
    for k in range(NS):
        beam = beam + beam_part(g.at[k], wts, (s + k) % NS)
    beam_finish(beam, lens, power)
    for k in range(OFFS):
        pltpu.make_async_copy(stage.at[k], vis.at[0, k, :, 0], osem.at[k]).wait()


def maths(int_lengths, beam_weights, gathered):
    return pl.pallas_call(
        math_kernel,
        out_shape=(
            jax.ShapeDtypeStruct((1, OFFS, INTEG, 1, 2, BLK, BLK), BF),
            jax.ShapeDtypeStruct((INTEG, 1, SHARE), F32),
        ),
        in_specs=[
            pl.BlockSpec(memory_space=pltpu.SMEM),
            pl.BlockSpec(memory_space=pl.ANY),
            pl.BlockSpec(memory_space=pltpu.VMEM),
        ],
        out_specs=(pl.BlockSpec(memory_space=pl.ANY), pl.BlockSpec(memory_space=pltpu.VMEM)),
        scratch_shapes=[
            pltpu.VMEM((2, SHARE, NS * BLK), BF),
            pltpu.VMEM((INTEG * BLK, 2 * SAMPLES), BF),
            pltpu.VMEM((OFFS, INTEG, 2, BLK, BLK), BF),
            pltpu.SemaphoreType.DMA,
            pltpu.SemaphoreType.DMA((OFFS,)),
        ],
        name="maths",
    )(int_lengths, beam_weights, gathered)


def local(voltages, phase_index, int_lengths, beam_weights):
    gathered = comm(phase_index, voltages)
    return maths(int_lengths, beam_weights, gathered)


def solution(mesh):
    return jax.shard_map(
        local,
        mesh=mesh,
        in_specs=(P(None, None, ("stn", "chan"), None), P(("stn", "chan")), P(), P()),
        out_specs=(P("stn", None, None, "chan", None, None, None), P(None, "chan", "stn")),
        check_vma=False,
    )
```

time: 169 us -> 55.2 us (0.33)
  Pallas kernels: 0 us -> 54.1 us
  loops' own time: 52 us -> 0 us
  waiting for transfers between devices: 44.1 us -> 0 us
  blocking collectives: 22.5 us -> 0 us
  between operations: 21.3 us -> 0.64 us
  local copies, waits for them, and re-layouts: 11.7 us -> 0 us
  other arithmetic: 9.31 us -> 0 us
  matrix products: 6.89 us -> 0 us
    pallas_call x0 -> x2, Pallas kernels: none -> 54.1 us  [the longest x1 48.6 us: comm(): pl.pallas_call(comm_kernel, out_shape=jax.ShapeDtypeStruct((NS, 2, LT, NC...]
    another operation x8 -> x0, loops' own time: 52 us -> none  [local(): lax.cond(offset <= halfway, place, leave, vis_total, other, offset)]
    all_gather x1 -> x0, waiting for transfers between devices: 44.1 us -> none  [local(): portion = lax.all_gather(turned, 'stn', axis=2, tiled=True)]
    all_to_all x1 -> x0, blocking collectives: 22.5 us -> none  [local(): lax.all_to_all(rotated, 'chan', split_axis=0, concat_axis=2, tiled=True)]
    dot_general x29 -> x0, matrix products: 6.89 us -> none  [the longest x20 4.83 us: correlate(): jnp.einsum('cal,cbl->cab', own_parts[period], segment, preferred_element_...]
    slice x9 -> x0, local copies, waits for them, and re-layouts: 6.37 us -> none  [the longest x5 3.38 us: correlate(): inverse = 1.0 / int_lengths[period].astype(jnp.float32)]
    dynamic_update_slice x5 -> x0, other arithmetic: 3.64 us -> none  [place(): lax.dynamic_update_slice(vis_total, fresh[None], (offset, 0, 0, 0, 0, 0))]
    lt x2 -> x0, other arithmetic: 2.3 us -> none  [windows(): keep_mask = (in_range < int_lengths[period])[None, None, :]]
  transfers between devices with their start and end apart: 1 -> 0, of which waited for: 1 -> 0; matrix products, arithmetic and copies ran while one was open for 3% -> 0% of each run, Pallas kernels for 0% -> 0%
where the time goes in v1:
time: 55.2 us; the launch traced here: 54.8 us
  Pallas kernels  54.1 us (98%)
  between operations  0.64 us (1%)
    pallas_call x1, Pallas kernels, comm(): pl.pallas_call(comm_kernel, out_shape=jax.ShapeDtypeStruct((NS, 2, LT, NC...  48.6 us
    pallas_call x1, Pallas kernels, maths(): pl.pallas_call(math_kernel, out_shape=(jax.ShapeDtypeStruct((1, OFFS, INT...  5.51 us

profile of v1, /device:TPU:1, one launch (start us, length us, event | category | flops | bytes accessed | tf_op | source)
XLA Modules:
  0.0 54.8 jit_solution(15810656850711801759)
XLA Ops:
  0.6 48.6 %comm.1.g_all = bf16[8,2,4,32,4,128]{5,4,3,2,1,0:T(4,128)(2,1)} custom-call(s32[4]{0:T(128)} %ph.1, bf16[32,2,4,512]{3,2,1,0:T(4,128)(2,1)} %v_hbm.1), custom_call_target="tpu_custom_call" | custom-call | tf_op jit(solution)/shard_map/comm/pallas_call | solution.py:112
  49.3 5.5 %maths.1 = (bf16[1,5,4,1,2,128,128]{6,5,4,3,2,1,0:T(8,128)(2,1)}, f32[4,1,32]{2,1,0:T(1,128)}) custom-call(s32[4]{0:T(128)} %lens.1, bf16[2,256,1024]{2,1,0:T(8,128)(2,1)} %w_hbm.1, bf16[8,2,4,32,4,128]{5,4,3,2,1,0:T(4,128)(2,1)} %comm.1.g_all), custom_call_target="tpu_custom_call" | custom-call | tf_op jit(solution)/shard_map/maths/pallas_call | solution.py:226

commit v2 on v1

v2 whole, which is shorter than its diff:
```python
import functools
import math

import jax
import jax.numpy as jnp
from jax import lax
from jax.experimental import pallas as pl
from jax.experimental.pallas import tpu as pltpu
from jax.sharding import PartitionSpec as P

INTEG = 4
BEAMS = 256
PHASES = 1024
NC = 32
NS = 8
LT = 4
SAMPLES = 512
BLK = 128
OFFS = 5
SHARE = BEAMS // NS
NCH = 4
W = LT // NCH
BF = jnp.bfloat16
F32 = jnp.float32
VMEM_LIMIT = 24 * 2**20
MESH = pl.DeviceIdType.MESH


def rotate_all(ph, vin, sbuf, trig):
    row = lax.broadcasted_iota(jnp.int32, (NC, 8, 128), 1)
    chan = lax.broadcasted_iota(jnp.int32, (NC, 8, 128), 0)
    col = row % 4
    step = jnp.where(col == 0, ph[0], jnp.where(col == 1, ph[1], jnp.where(col == 2, ph[2], ph[3])))
    turns = chan * step - jnp.where(row >= 4, PHASES // 4, 0)
    turns = ((turns + PHASES // 2) & (PHASES - 1)) - PHASES // 2
    trig[...] = jnp.cos(turns.astype(F32) * (2.0 * math.pi / PHASES))

    def one(c, carry):
        cs = trig[c]
        cos, sin = cs[0:4], cs[4:8]
        re = vin[c, 0].astype(F32)
        im = vin[c, 1].astype(F32)
        for t in range(LT):
            a = re[:, t * 128 : (t + 1) * 128]
            b = im[:, t * 128 : (t + 1) * 128]
            sbuf[c, 0, t] = (a * cos + b * sin).astype(BF)
            sbuf[c, 1, t] = (b * cos - a * sin).astype(BF)
        return carry

    lax.fori_loop(0, NC, one, 0, unroll=4)


def window_edges(lens):
    edges = [jnp.int32(0)]
    for j in range(INTEG):
        edges.append(edges[-1] + lens[j])
    return edges


def build_windows(blk, lens, left):
    edges = window_edges(lens)
    lane = lax.broadcasted_iota(jnp.int32, (1, 128), 1)
    for t in range(LT):
        at = lane + t * 128
        for j in range(INTEG):
            keep = ((at >= edges[j]) & (at < edges[j + 1])).astype(F32).astype(BF)
            for p in range(2):
                left[j * BLK : (j + 1) * BLK, (p * LT + t) * 128 : (p * LT + t + 1) * 128] = (
                    blk[p, t] * keep
                )


def correlate(blk, lens, left, put):
    re = [blk[0, t] for t in range(LT)]
    im = [blk[1, t] for t in range(LT)]
    neg = [-x for x in im]
    right = jnp.concatenate(
        [jnp.concatenate(re + im, axis=1), jnp.concatenate(neg + re, axis=1)], axis=0
    )
    prod = lax.dot_general(
        left[...], right, (((1,), (1,)), ((), ())), preferred_element_type=F32
    )
    for j in range(INTEG):
        inverse = 1.0 / jnp.full((1, 128), lens[j], jnp.int32).astype(F32)
        for p in range(2):
            put(j, p, (prod[j * BLK : (j + 1) * BLK, p * 128 : (p + 1) * 128] * inverse).astype(BF))


def beam_part(blk, wts, q):
    cols = pl.ds(pl.multiple_of(q * BLK, BLK), BLK)
    wr = wts[0, :, cols]
    wi = wts[1, :, cols]
    stack = jnp.concatenate(
        [jnp.concatenate([wr, -wi], axis=1), jnp.concatenate([wi, wr], axis=1)], axis=0
    )
    parts = []
    for t in range(0, LT, 2):
        x = jnp.concatenate(
            [jnp.concatenate([blk[p, t], blk[p, t + 1]], axis=1) for p in range(2)], axis=0
        )
        parts.append(jnp.dot(stack, x, preferred_element_type=F32))
    return jnp.concatenate(parts, axis=1)


def beam_finish(beam, lens, out):
    power = beam[:SHARE] ** 2 + beam[SHARE:] ** 2
    edges = window_edges(lens)
    at = lax.broadcasted_iota(jnp.int32, (8, SAMPLES), 1)
    row = lax.broadcasted_iota(jnp.int32, (8, SAMPLES), 0)
    mask = jnp.zeros((8, SAMPLES), F32)
    for j in range(INTEG):
        inside = (row == j) & (at >= edges[j]) & (at < edges[j + 1])
        mask = jnp.where(inside, 1.0, mask)
    total = lax.dot_general(
        mask, power, (((1,), (1,)), ((), ())), precision=lax.Precision.HIGHEST,
        preferred_element_type=F32,
    )
    for j in range(INTEG):
        out[j] = total[j : j + 1] / jnp.full((1, SHARE), lens[j], jnp.int32).astype(F32)


UP, DOWN, ACROSS = (0, 1), (0, -1), (1, 0)
FIRST = ((0, 4, ACROSS), (0, 1, UP), (0, 3, DOWN))


def second(q):
    if q % 2 == 0:
        return ((3, 7, ACROSS), (1, 2, UP), (4, 5, UP))
    return ((1, 5, ACROSS), (3, 2, DOWN), (4, 7, DOWN))


def third(q):
    return ((5, 6, UP), (7, 6, DOWN), (2, 6, ACROSS), (2, 6, ACROSS))[q]


def kernel(
    ph_hbm, lens_hbm, v_hbm, w_hbm, vis, power,
    ph, lens, g, vin, sbuf, trig, wts, left, stage, beam, lsem, s1, r1, s2, r2, osem,
):
    c = lax.axis_index("chan")
    s = lax.axis_index("stn")
    h, y = s // 4, s % 4

    def to(step):
        return {"chan": c, "stn": ((h + step[0]) % 2) * 4 + (y + step[1] + 4) % 4}

    barrier = pltpu.get_barrier_semaphore()

    def hello(k, carry):
        pl.semaphore_signal(
            barrier, 1, device_id={"chan": (c + k) % NC, "stn": s}, device_id_type=MESH
        )
        return carry

    lax.fori_loop(1, NC, hello, 0)
    for step in (UP, DOWN, ACROSS):
        pl.semaphore_signal(barrier, 1, device_id=to(step), device_id_type=MESH)
    load = pltpu.make_async_copy(v_hbm, vin, lsem.at[0])
    load.start()
    load_p = pltpu.make_async_copy(ph_hbm, ph, lsem.at[3])
    load_p.start()
    load_l = pltpu.make_async_copy(lens_hbm, lens, lsem.at[4])
    load_l.start()
    load_w = pltpu.make_async_copy(
        w_hbm.at[:, pl.ds(pl.multiple_of(s * SHARE, SHARE), SHARE)], wts, lsem.at[2]
    )
    load_w.start()
    load_p.wait()
    load.wait()
    rotate_all(ph, vin, sbuf, trig)
    pl.semaphore_wait(barrier, NC - 1 + 3)

    def span(q):
        return pl.ds(q * W, W)

    for q in range(NCH):

        def send(k, carry):
            d = (c + k) % NC
            pltpu.make_async_remote_copy(
                sbuf.at[d, :, span(q)], g.at[0, :, span(q), c], s1.at[q], r1.at[q],
                device_id={"chan": d, "stn": s}, device_id_type=MESH,
            ).start()
            return carry

        lax.fori_loop(1, NC, send, 0)
    own = pltpu.make_async_copy(sbuf.at[c], g.at[0, :, :, c], lsem.at[1])
    own.start()
    own.wait()
    load_w.wait()
    load_l.wait()

    sends = []
    have = {0: NCH}

    def copy(src, dst, q, step):
        return pltpu.make_async_remote_copy(
            g.at[src, :, span(q)], g.at[dst, :, span(q)], s2.at[dst, q], r2.at[dst, q],
            device_id=to(step), device_id_type=MESH,
        )

    def arrive(slot, upto):
        while have.get(slot, 0) < upto:
            q = have.get(slot, 0)
            copy(0, slot, q, UP).wait_recv()
            have[slot] = q + 1

    def push(src, dst, step, q):
        arrive(src, q + 1)
        cp = copy(src, dst, q, step)
        cp.start()
        sends.append(cp)

    blocks = g.reshape(NS, 2, LT, BLK, 128)

    def process(slot):
        arrive(slot, NCH)
        dh, dy = slot // 4, slot % 4
        q = ((h + dh) % 2) * 4 + (y - dy + 4) % 4
        k = (q - s + NS) % NS
        part = beam_part(blocks.at[slot], wts, q)
        beam[...] = part if slot == 0 else beam[...] + part

        def vis_block():
            def put(j, p, value):
                stage[k, j, p] = value

            correlate(blocks.at[slot], lens, left, put)
            pltpu.make_async_copy(stage.at[k], vis.at[0, k, :, 0], osem.at[k]).start()

        if slot == 0:
            vis_block()
        else:
            pl.when(k < OFFS)(vis_block)

    for q in range(NCH):
        turned = pltpu.make_async_remote_copy(
            sbuf.at[pl.ds(0, NC - 1), :, span(q)], g.at[0, :, span(q), pl.ds(0, NC - 1)],
            s1.at[q], r1.at[q], device_id=to(UP), device_id_type=MESH,
        )
        turned.wait_recv()
        for src, dst, step in FIRST:
            push(src, dst, step, q)
        turned.wait_send()
    build_windows(blocks.at[0], lens, left)
    process(0)
    for q in range(NCH):
        for src, dst, step in second(q):
            push(src, dst, step, q)
    for slot in (4, 1, 3):
        process(slot)
    for q in range(NCH):
        push(*third(q), q)
    for slot in (2, 5, 7, 6):
        process(slot)
    beam_finish(beam[...], lens, power)
    for cp in sends:
        cp.wait_send()
    for k in range(OFFS):
        pltpu.make_async_copy(stage.at[k], vis.at[0, k, :, 0], osem.at[k]).wait()


def local(voltages, phase_index, int_lengths, beam_weights):
    return pl.pallas_call(
        kernel,
        out_shape=(
            jax.ShapeDtypeStruct((1, OFFS, INTEG, 1, 2, BLK, BLK), BF),
            jax.ShapeDtypeStruct((INTEG, 1, SHARE), F32),
        ),
        in_specs=[
            pl.BlockSpec(memory_space=pltpu.HBM),
            pl.BlockSpec(memory_space=pltpu.HBM),
            pl.BlockSpec(memory_space=pltpu.HBM),
            pl.BlockSpec(memory_space=pltpu.HBM),
        ],
        out_specs=(pl.BlockSpec(memory_space=pl.ANY), pl.BlockSpec(memory_space=pltpu.VMEM)),
        scratch_shapes=[
            pltpu.SMEM((INTEG,), jnp.int32),
            pltpu.SMEM((INTEG,), jnp.int32),
            pltpu.VMEM((NS, 2, LT, NC, 4, 128), BF),
            pltpu.VMEM((NC, 2, 4, SAMPLES), BF),
            pltpu.VMEM((NC, 2, LT, 4, 128), BF),
            pltpu.VMEM((NC, 8, 128), F32),
            pltpu.VMEM((2, SHARE, NS * BLK), BF),
            pltpu.VMEM((INTEG * BLK, 2 * SAMPLES), BF),
            pltpu.VMEM((OFFS, INTEG, 2, BLK, BLK), BF),
            pltpu.VMEM((2 * SHARE, SAMPLES), F32),
            pltpu.SemaphoreType.DMA((5,)),
            pltpu.SemaphoreType.DMA((NCH,)),
            pltpu.SemaphoreType.DMA((NCH,)),
            pltpu.SemaphoreType.DMA((NS, NCH)),
            pltpu.SemaphoreType.DMA((NS, NCH)),
            pltpu.SemaphoreType.DMA((OFFS,)),
        ],
        compiler_params=pltpu.CompilerParams(
            collective_id=0, has_side_effects=True, vmem_limit_bytes=VMEM_LIMIT
        ),
        name="correlator",
    )(
        *[
            pltpu.with_memory_space_constraint(x, pltpu.HBM)
            for x in (phase_index, int_lengths, voltages, beam_weights)
        ]
    )


def solution(mesh):
    return jax.shard_map(
        local,
        mesh=mesh,
        in_specs=(P(None, None, ("stn", "chan"), None), P(("stn", "chan")), P(), P()),
        out_specs=(P("stn", None, None, "chan", None, None, None), P(None, "chan", "stn")),
        check_vma=False,
    )
```

time: 55.2 us -> 36.7 us (0.66)
  Pallas kernels: 54.1 us -> 34.4 us
  local copies, waits for them, and re-layouts: 0 us -> 1.64 us
    pallas_call x2 -> x1, Pallas kernels: 54.1 us -> 34.4 us  [local(): pl.pallas_call(kernel, out_shape=(jax.ShapeDtypeStruct((1, OFFS, INTEG, 1...]
    unnamed x0 -> x2, local copies, waits for them, and re-layouts: none -> 1.64 us
where the time goes in v2:
time: 36.7 us; the launch traced here: 36.6 us
  Pallas kernels  34.4 us (94%)
  local copies, waits for them, and re-layouts  1.64 us (4%)
  between operations  0.64 us (2%)
    pallas_call x1, Pallas kernels, local(): pl.pallas_call(kernel, out_shape=(jax.ShapeDtypeStruct((1, OFFS, INTEG, 1...  34.4 us
    unnamed x2, local copies, waits for them, and re-layouts  1.64 us

profile of v2, /device:TPU:1, one launch (start us, length us, event | category | flops | bytes accessed | tf_op | source)
XLA Modules:
  0.0 36.6 jit_solution(17375120034894280476)
XLA Ops:
  0.6 34.4 %correlator.1 = (bf16[1,5,4,1,2,128,128]{6,5,4,3,2,1,0:T(8,128)(2,1)S(1)}, f32[4,1,32]{2,1,0:T(1,128)S(1)}) custom-call(s32[4]{0:T(128)} %ph_hbm.1, s32[4]{0:T(128)} %lens_hbm.1, bf16[32,2,4,512]{3,2,1,0:T(4,128)(2,1)} %v_hbm.1, bf16[2,256,1024]{2,1,0:T(8,128)(2,1)} %w_hbm.1), custom_call_target="tpu_custom_call" | custom-call | tf_op jit(solution)/shard_map/correlator/pallas_call | solution.py:264
  35.0 1.1 %copy.8 = bf16[1,5,4,1,2,128,128]{6,5,4,3,2,1,0:T(8,128)(2,1)} copy(bf16[1,5,4,1,2,128,128]{6,5,4,3,2,1,0:T(8,128)(2,1)S(1)} %get-tuple-element.4) | data formatting | bytes 2621440
  36.1 0.6 %copy.9 = f32[4,1,32]{2,1,0:T(1,128)} copy(f32[4,1,32]{2,1,0:T(1,128)S(1)} %get-tuple-element.5) | data formatting | bytes 1024

commit v3 on v2

--- a/solution.py
+++ b/solution.py
@@ -18,9 +18,9 @@
 BLK = 128
 OFFS = 5
 SHARE = BEAMS // NS
-NCH = 4
-W = LT // NCH
+NCH = LT
 BF = jnp.bfloat16
+FAR = sorted(range(1, NC), key=lambda k: -min(k % 16, 16 - k % 16))
 F32 = jnp.float32
 VMEM_LIMIT = 24 * 2**20
 MESH = pl.DeviceIdType.MESH
@@ -43,8 +43,8 @@
         for t in range(LT):
             a = re[:, t * 128 : (t + 1) * 128]
             b = im[:, t * 128 : (t + 1) * 128]
-            sbuf[c, 0, t] = (a * cos + b * sin).astype(BF)
-            sbuf[c, 1, t] = (b * cos - a * sin).astype(BF)
+            sbuf[t, c, 0] = (a * cos + b * sin).astype(BF)
+            sbuf[t, c, 1] = (b * cos - a * sin).astype(BF)
         return carry
 
     lax.fori_loop(0, NC, one, 0, unroll=4)
@@ -70,23 +70,30 @@
                 )
 
 
-def correlate(blk, lens, left, put):
-    re = [blk[0, t] for t in range(LT)]
-    im = [blk[1, t] for t in range(LT)]
+def products(blk, left, lo, hi):
+    re = [blk[0, t] for t in range(lo, hi)]
+    im = [blk[1, t] for t in range(lo, hi)]
     neg = [-x for x in im]
     right = jnp.concatenate(
         [jnp.concatenate(re + im, axis=1), jnp.concatenate(neg + re, axis=1)], axis=0
     )
-    prod = lax.dot_general(
-        left[...], right, (((1,), (1,)), ((), ())), preferred_element_type=F32
-    )
+    if (lo, hi) == (0, LT):
+        rows = left[...]
+    else:
+        rows = jnp.concatenate(
+            [left[:, (p * LT + lo) * 128 : (p * LT + hi) * 128] for p in range(2)], axis=1
+        )
+    return lax.dot_general(rows, right, (((1,), (1,)), ((), ())), preferred_element_type=F32)
+
+
+def average(prod, lens, put):
     for j in range(INTEG):
         inverse = 1.0 / jnp.full((1, 128), lens[j], jnp.int32).astype(F32)
         for p in range(2):
             put(j, p, (prod[j * BLK : (j + 1) * BLK, p * 128 : (p + 1) * 128] * inverse).astype(BF))
 
 
-def beam_part(blk, wts, q):
+def beam_part(blk, wts, q, lo, hi):
     cols = pl.ds(pl.multiple_of(q * BLK, BLK), BLK)
     wr = wts[0, :, cols]
     wi = wts[1, :, cols]
@@ -94,29 +101,29 @@
         [jnp.concatenate([wr, -wi], axis=1), jnp.concatenate([wi, wr], axis=1)], axis=0
     )
     parts = []
-    for t in range(0, LT, 2):
+    for t in range(lo, hi, 2):
         x = jnp.concatenate(
-            [jnp.concatenate([blk[p, t], blk[p, t + 1]], axis=1) for p in range(2)], axis=0
+            [jnp.concatenate([blk[p, u] for u in range(t, min(t + 2, hi))], axis=1) for p in range(2)],
+            axis=0,
         )
         parts.append(jnp.dot(stack, x, preferred_element_type=F32))
     return jnp.concatenate(parts, axis=1)
 
 
-def beam_finish(beam, lens, out):
+def window_powers(beam, lens, lo):
     power = beam[:SHARE] ** 2 + beam[SHARE:] ** 2
+    width = beam.shape[1]
     edges = window_edges(lens)
-    at = lax.broadcasted_iota(jnp.int32, (8, SAMPLES), 1)
-    row = lax.broadcasted_iota(jnp.int32, (8, SAMPLES), 0)
-    mask = jnp.zeros((8, SAMPLES), F32)
+    at = lax.broadcasted_iota(jnp.int32, (8, width), 1) + lo * 128
+    row = lax.broadcasted_iota(jnp.int32, (8, width), 0)
+    mask = jnp.zeros((8, width), F32)
     for j in range(INTEG):
         inside = (row == j) & (at >= edges[j]) & (at < edges[j + 1])
         mask = jnp.where(inside, 1.0, mask)
-    total = lax.dot_general(
+    return lax.dot_general(
         mask, power, (((1,), (1,)), ((), ())), precision=lax.Precision.HIGHEST,
         preferred_element_type=F32,
     )
-    for j in range(INTEG):
-        out[j] = total[j : j + 1] / jnp.full((1, SHARE), lens[j], jnp.int32).astype(F32)
 
 
 UP, DOWN, ACROSS = (0, 1), (0, -1), (1, 0)
@@ -135,7 +142,7 @@
 
 def kernel(
     ph_hbm, lens_hbm, v_hbm, w_hbm, vis, power,
-    ph, lens, g, vin, sbuf, trig, wts, left, stage, beam, lsem, s1, r1, s2, r2, osem,
+    ph, lens, g, vin, sbuf, trig, wts, left, beam, acc, sums, lsem, o1, s1, r1, s2, r2,
 ):
     c = lax.axis_index("chan")
     s = lax.axis_index("stn")
@@ -146,13 +153,10 @@
 
     barrier = pltpu.get_barrier_semaphore()
 
-    def hello(k, carry):
+    for k in FAR:
         pl.semaphore_signal(
             barrier, 1, device_id={"chan": (c + k) % NC, "stn": s}, device_id_type=MESH
         )
-        return carry
-
-    lax.fori_loop(1, NC, hello, 0)
     for step in (UP, DOWN, ACROSS):
         pl.semaphore_signal(barrier, 1, device_id=to(step), device_id_type=MESH)
     load = pltpu.make_async_copy(v_hbm, vin, lsem.at[0])
@@ -170,23 +174,20 @@
     rotate_all(ph, vin, sbuf, trig)
     pl.semaphore_wait(barrier, NC - 1 + 3)
 
-    def span(q):
-        return pl.ds(q * W, W)
-
     for q in range(NCH):
-
-        def send(k, carry):
+        for k in FAR:
             d = (c + k) % NC
             pltpu.make_async_remote_copy(
-                sbuf.at[d, :, span(q)], g.at[0, :, span(q), c], s1.at[q], r1.at[q],
+                sbuf.at[q, d], g.at[0, :, q, c], s1.at[q], r1.at[q],
                 device_id={"chan": d, "stn": s}, device_id_type=MESH,
             ).start()
-            return carry
-
-        lax.fori_loop(1, NC, send, 0)
-    own = pltpu.make_async_copy(sbuf.at[c], g.at[0, :, :, c], lsem.at[1])
-    own.start()
-    own.wait()
+    owns = [
+        pltpu.make_async_copy(sbuf.at[q, c], g.at[0, :, q, c], o1.at[q]) for q in range(NCH)
+    ]
+    for cp in owns:
+        cp.start()
+    for cp in owns:
+        cp.wait()
     load_w.wait()
     load_l.wait()
 
@@ -195,7 +196,7 @@
 
     def copy(src, dst, q, step):
         return pltpu.make_async_remote_copy(
-            g.at[src, :, span(q)], g.at[dst, :, span(q)], s2.at[dst, q], r2.at[dst, q],
+            g.at[src, :, q], g.at[dst, :, q], s2.at[dst, q], r2.at[dst, q],
             device_id=to(step), device_id_type=MESH,
         )
 
@@ -213,30 +214,55 @@
 
     blocks = g.reshape(NS, 2, LT, BLK, 128)
 
+    def block_at(slot):
+        dh, dy = slot // 4, slot % 4
+        q = ((h + dh) % 2) * 4 + (y - dy + 4) % 4
+        return q, (q - s + NS) % NS
+
     def process(slot):
         arrive(slot, NCH)
-        dh, dy = slot // 4, slot % 4
-        q = ((h + dh) % 2) * 4 + (y - dy + 4) % 4
-        k = (q - s + NS) % NS
-        part = beam_part(blocks.at[slot], wts, q)
+        q, k = block_at(slot)
+        part = beam_part(blocks.at[slot], wts, q, 0, LT)
         beam[...] = part if slot == 0 else beam[...] + part
 
         def vis_block():
             def put(j, p, value):
-                stage[k, j, p] = value
-
-            correlate(blocks.at[slot], lens, left, put)
-            pltpu.make_async_copy(stage.at[k], vis.at[0, k, :, 0], osem.at[k]).start()
+                vis[0, k, j, 0, p] = value
+
+            average(products(blocks.at[slot], left, 0, LT), lens, put)
 
         if slot == 0:
             vis_block()
         else:
             pl.when(k < OFFS)(vis_block)
 
+    def process_last(slot, cut):
+        q, k = block_at(slot)
+        arrive(slot, cut)
+
+        @pl.when(k < OFFS)
+        def _():
+            acc[...] = products(blocks.at[slot], left, 0, cut)
+
+        head = beam[:, : cut * 128] + beam_part(blocks.at[slot], wts, q, 0, cut)
+        sums[...] = window_powers(head, lens, 0)
+        arrive(slot, NCH)
+        rest = beam[:, cut * 128 :] + beam_part(blocks.at[slot], wts, q, cut, LT)
+        total = sums[...] + window_powers(rest, lens, cut)
+        for j in range(INTEG):
+            power[j] = total[j : j + 1] / jnp.full((1, SHARE), lens[j], jnp.int32).astype(F32)
+
+        @pl.when(k < OFFS)
+        def _():
+            def put(j, p, value):
+                vis[0, k, j, 0, p] = value
+
+            average(acc[...] + products(blocks.at[slot], left, cut, LT), lens, put)
+
     for q in range(NCH):
         turned = pltpu.make_async_remote_copy(
-            sbuf.at[pl.ds(0, NC - 1), :, span(q)], g.at[0, :, span(q), pl.ds(0, NC - 1)],
-            s1.at[q], r1.at[q], device_id=to(UP), device_id_type=MESH,
+            sbuf.at[q, pl.ds(0, NC - 1)], g.at[0, :, q, pl.ds(0, NC - 1)], s1.at[q], r1.at[q],
+            device_id=to(UP), device_id_type=MESH,
         )
         turned.wait_recv()
         for src, dst, step in FIRST:
@@ -251,17 +277,41 @@
         process(slot)
     for q in range(NCH):
         push(*third(q), q)
-    for slot in (2, 5, 7, 6):
+    for slot in (2, 5, 7):
         process(slot)
-    beam_finish(beam[...], lens, power)
+    process_last(6, LT - 1)
     for cp in sends:
         cp.wait_send()
-    for k in range(OFFS):
-        pltpu.make_async_copy(stage.at[k], vis.at[0, k, :, 0], osem.at[k]).wait()
+
+
+def store_kernel(vis_in, power_in, vis, power, sem):
+    copies = [
+        pltpu.make_async_copy(vis_in, vis, sem.at[0]),
+        pltpu.make_async_copy(power_in, power, sem.at[1]),
+    ]
+    for cp in copies:
+        cp.start()
+    for cp in copies:
+        cp.wait()
+
+
+def store(vis, power):
+    return pl.pallas_call(
+        store_kernel,
+        out_shape=(
+            jax.ShapeDtypeStruct(vis.shape, vis.dtype),
+            jax.ShapeDtypeStruct(power.shape, power.dtype),
+        ),
+        in_specs=[pl.BlockSpec(memory_space=pl.ANY)] * 2,
+        out_specs=(pl.BlockSpec(memory_space=pltpu.HBM), pl.BlockSpec(memory_space=pltpu.HBM)),
+        scratch_shapes=[pltpu.SemaphoreType.DMA((2,))],
+        compiler_params=pltpu.CompilerParams(vmem_limit_bytes=VMEM_LIMIT),
+        name="store",
+    )(vis, power)
 
 
 def local(voltages, phase_index, int_lengths, beam_weights):
-    return pl.pallas_call(
+    vis, power = pl.pallas_call(
         kernel,
         out_shape=(
             jax.ShapeDtypeStruct((1, OFFS, INTEG, 1, 2, BLK, BLK), BF),
@@ -273,24 +323,25 @@
             pl.BlockSpec(memory_space=pltpu.HBM),
             pl.BlockSpec(memory_space=pltpu.HBM),
         ],
-        out_specs=(pl.BlockSpec(memory_space=pl.ANY), pl.BlockSpec(memory_space=pltpu.VMEM)),
+        out_specs=(pl.BlockSpec(memory_space=pltpu.VMEM), pl.BlockSpec(memory_space=pltpu.VMEM)),
         scratch_shapes=[
             pltpu.SMEM((INTEG,), jnp.int32),
             pltpu.SMEM((INTEG,), jnp.int32),
             pltpu.VMEM((NS, 2, LT, NC, 4, 128), BF),
             pltpu.VMEM((NC, 2, 4, SAMPLES), BF),
-            pltpu.VMEM((NC, 2, LT, 4, 128), BF),
+            pltpu.VMEM((LT, NC, 2, 4, 128), BF),
             pltpu.VMEM((NC, 8, 128), F32),
             pltpu.VMEM((2, SHARE, NS * BLK), BF),
             pltpu.VMEM((INTEG * BLK, 2 * SAMPLES), BF),
-            pltpu.VMEM((OFFS, INTEG, 2, BLK, BLK), BF),
             pltpu.VMEM((2 * SHARE, SAMPLES), F32),
+            pltpu.VMEM((INTEG * BLK, 2 * BLK), F32),
+            pltpu.VMEM((8, SHARE), F32),
             pltpu.SemaphoreType.DMA((5,)),
+            pltpu.SemaphoreType.DMA((NCH,)),
             pltpu.SemaphoreType.DMA((NCH,)),
             pltpu.SemaphoreType.DMA((NCH,)),
             pltpu.SemaphoreType.DMA((NS, NCH)),
             pltpu.SemaphoreType.DMA((NS, NCH)),
-            pltpu.SemaphoreType.DMA((OFFS,)),
         ],
         compiler_params=pltpu.CompilerParams(
             collective_id=0, has_side_effects=True, vmem_limit_bytes=VMEM_LIMIT
@@ -302,6 +353,7 @@
             for x in (phase_index, int_lengths, voltages, beam_weights)
         ]
     )
+    return store(vis, power)
 
 
 def solution(mesh):

time: 36.7 us -> 35.1 us (0.956)
  local copies, waits for them, and re-layouts: 1.64 us -> 0 us
    unnamed x2 -> x0, local copies, waits for them, and re-layouts: 1.64 us -> none
    pallas_call x0 -> x1, Pallas kernels: none -> 1.08 us  [store(): pl.pallas_call(store_kernel, out_shape=(jax.ShapeDtypeStruct(vis.shape, v...]
    pallas_call x1, Pallas kernels: 34.4 us -> 33.3 us  [local(): pl.pallas_call(kernel, out_shape=(jax.ShapeDtypeStruct((1, OFFS, INTEG, 1...]
where the time goes in v3:
time: 35.1 us; the launch traced here: 35 us
  Pallas kernels  34.4 us (98%)
  between operations  0.64 us (2%)
    pallas_call x1, Pallas kernels, local(): pl.pallas_call(kernel, out_shape=(jax.ShapeDtypeStruct((1, OFFS, INTEG, 1...  33.3 us
    pallas_call x1, Pallas kernels, store(): pl.pallas_call(store_kernel, out_shape=(jax.ShapeDtypeStruct(vis.shape, v...  1.08 us

profile of v3, /device:TPU:1, one launch (start us, length us, event | category | flops | bytes accessed | tf_op | source)
XLA Modules:
  0.0 35.0 jit_solution(9318482936583498387)
XLA Ops:
  0.6 33.3 %correlator.1 = (bf16[1,5,4,1,2,128,128]{6,5,4,3,2,1,0:T(8,128)(2,1)S(1)}, f32[4,1,32]{2,1,0:T(1,128)S(1)}) custom-call(s32[4]{0:T(128)} %ph_hbm.1, s32[4]{0:T(128)} %lens_hbm.1, bf16[32,2,4,512]{3,2,1,0:T(4,128)(2,1)} %v_hbm.1, bf16[2,256,1024]{2,1,0:T(8,128)(2,1)} %w_hbm.1), custom_call_target="tpu_custom_call" | custom-call | tf_op jit(solution)/shard_map/correlator/pallas_call | solution.py:314
  34.0 1.1 %store.1 = (bf16[1,5,4,1,2,128,128]{6,5,4,3,2,1,0:T(8,128)(2,1)}, f32[4,1,32]{2,1,0:T(1,128)}) custom-call(bf16[1,5,4,1,2,128,128]{6,5,4,3,2,1,0:T(8,128)(2,1)S(1)} %get-tuple-element.4.vis_in, f32[4,1,32]{2,1,0:T(1,128)S(1)} %get-tuple-element.5.power_in), custom_call_target="tpu_custom_call" | custom-call | tf_op jit(solution)/shard_map/store/pallas_call | solution.py:299

commit v4 on v3

--- a/solution.py
+++ b/solution.py
@@ -93,13 +93,15 @@
             put(j, p, (prod[j * BLK : (j + 1) * BLK, p * 128 : (p + 1) * 128] * inverse).astype(BF))
 
 
-def beam_part(blk, wts, q, lo, hi):
+def beam_part(blk, wts, dests, q, lo, hi):
     cols = pl.ds(pl.multiple_of(q * BLK, BLK), BLK)
-    wr = wts[0, :, cols]
-    wi = wts[1, :, cols]
-    stack = jnp.concatenate(
-        [jnp.concatenate([wr, -wi], axis=1), jnp.concatenate([wi, wr], axis=1)], axis=0
-    )
+    rows = []
+    for d in dests:
+        wr = wts[d, 0, :, cols]
+        wi = wts[d, 1, :, cols]
+        rows.append(jnp.concatenate([wr, -wi], axis=1))
+        rows.append(jnp.concatenate([wi, wr], axis=1))
+    stack = jnp.concatenate(rows, axis=0)
     parts = []
     for t in range(lo, hi, 2):
         x = jnp.concatenate(
@@ -128,21 +130,12 @@
 
 UP, DOWN, ACROSS = (0, 1), (0, -1), (1, 0)
 FIRST = ((0, 4, ACROSS), (0, 1, UP), (0, 3, DOWN))
-
-
-def second(q):
-    if q % 2 == 0:
-        return ((3, 7, ACROSS), (1, 2, UP), (4, 5, UP))
-    return ((1, 5, ACROSS), (3, 2, DOWN), (4, 7, DOWN))
-
-
-def third(q):
-    return ((5, 6, UP), (7, 6, DOWN), (2, 6, ACROSS), (2, 6, ACROSS))[q]
+ROWS = 2 * SHARE
 
 
 def kernel(
     ph_hbm, lens_hbm, v_hbm, w_hbm, vis, power,
-    ph, lens, g, vin, sbuf, trig, wts, left, beam, acc, sums, lsem, o1, s1, r1, s2, r2,
+    ph, lens, g, vin, sbuf, trig, wts, left, beam, acc, sums, out_part, in_part, lsem, o1, s1, r1, s2, r2, s3, r3,
 ):
     c = lax.axis_index("chan")
     s = lax.axis_index("stn")
@@ -159,20 +152,28 @@
         )
     for step in (UP, DOWN, ACROSS):
         pl.semaphore_signal(barrier, 1, device_id=to(step), device_id_type=MESH)
+    for k in (2, NS - 2):
+        pl.semaphore_signal(
+            barrier, 1, device_id={"chan": c, "stn": (s + k) % NS}, device_id_type=MESH
+        )
     load = pltpu.make_async_copy(v_hbm, vin, lsem.at[0])
     load.start()
     load_p = pltpu.make_async_copy(ph_hbm, ph, lsem.at[3])
     load_p.start()
     load_l = pltpu.make_async_copy(lens_hbm, lens, lsem.at[4])
     load_l.start()
-    load_w = pltpu.make_async_copy(
-        w_hbm.at[:, pl.ds(pl.multiple_of(s * SHARE, SHARE), SHARE)], wts, lsem.at[2]
-    )
-    load_w.start()
+    load_w = [
+        pltpu.make_async_copy(
+            w_hbm.at[:, pl.ds(pl.multiple_of(d * SHARE, SHARE), SHARE)], wts.at[i], lsem.at[i + 1]
+        )
+        for i, d in enumerate((s, (s + 2) % NS))
+    ]
+    for cp in load_w:
+        cp.start()
     load_p.wait()
     load.wait()
     rotate_all(ph, vin, sbuf, trig)
-    pl.semaphore_wait(barrier, NC - 1 + 3)
+    pl.semaphore_wait(barrier, NC - 1 + 5)
 
     for q in range(NCH):
         for k in FAR:
@@ -188,11 +189,12 @@
         cp.start()
     for cp in owns:
         cp.wait()
-    load_w.wait()
+    for cp in load_w:
+        cp.wait()
     load_l.wait()
 
     sends = []
-    have = {0: NCH}
+    have = {(0, q) for q in range(NCH)}
 
     def copy(src, dst, q, step):
         return pltpu.make_async_remote_copy(
@@ -200,14 +202,14 @@
             device_id=to(step), device_id_type=MESH,
         )
 
-    def arrive(slot, upto):
-        while have.get(slot, 0) < upto:
-            q = have.get(slot, 0)
-            copy(0, slot, q, UP).wait_recv()
-            have[slot] = q + 1
+    def arrive(slot, *chunks):
+        for q in chunks:
+            if (slot, q) not in have:
+                copy(0, slot, q, UP).wait_recv()
+                have.add((slot, q))
 
     def push(src, dst, step, q):
-        arrive(src, q + 1)
+        arrive(src, q)
         cp = copy(src, dst, q, step)
         cp.start()
         sends.append(cp)
@@ -220,44 +222,31 @@
         return q, (q - s + NS) % NS
 
     def process(slot):
-        arrive(slot, NCH)
+        arrive(slot, *range(NCH))
         q, k = block_at(slot)
-        part = beam_part(blocks.at[slot], wts, q, 0, LT)
-        beam[...] = part if slot == 0 else beam[...] + part
-
-        def vis_block():
-            def put(j, p, value):
-                vis[0, k, j, 0, p] = value
-
-            average(products(blocks.at[slot], left, 0, LT), lens, put)
-
-        if slot == 0:
-            vis_block()
-        else:
-            pl.when(k < OFFS)(vis_block)
-
-    def process_last(slot, cut):
-        q, k = block_at(slot)
-        arrive(slot, cut)
+        part = beam_part(blocks.at[slot], wts, (0,), q, 0, LT)
+        beam[...] += part
 
         @pl.when(k < OFFS)
         def _():
-            acc[...] = products(blocks.at[slot], left, 0, cut)
-
-        head = beam[:, : cut * 128] + beam_part(blocks.at[slot], wts, q, 0, cut)
-        sums[...] = window_powers(head, lens, 0)
-        arrive(slot, NCH)
-        rest = beam[:, cut * 128 :] + beam_part(blocks.at[slot], wts, q, cut, LT)
-        total = sums[...] + window_powers(rest, lens, cut)
-        for j in range(INTEG):
-            power[j] = total[j : j + 1] / jnp.full((1, SHARE), lens[j], jnp.int32).astype(F32)
-
-        @pl.when(k < OFFS)
-        def _():
-            def put(j, p, value):
-                vis[0, k, j, 0, p] = value
-
-            average(acc[...] + products(blocks.at[slot], left, cut, LT), lens, put)
+            vis_block(slot, k)
+
+    def vis_block(slot, k):
+        def put(j, p, value):
+            vis[0, k, j, 0, p] = value
+
+        average(products(blocks.at[slot], left, 0, LT), lens, put)
+
+    middle = (y == 1) | (y == 2)
+    part_copy = pltpu.make_async_remote_copy(
+        out_part, in_part, s3, r3,
+        device_id={"chan": c, "stn": (s + 2) % NS}, device_id_type=MESH,
+    )
+
+    spare_copy = pltpu.make_async_remote_copy(
+        g.at[3, :, 2], g.at[2, :, 2], s2.at[6, 0], r2.at[2, 2],
+        device_id=to(DOWN), device_id_type=MESH,
+    )
 
     for q in range(NCH):
         turned = pltpu.make_async_remote_copy(
@@ -268,20 +257,85 @@
         for src, dst, step in FIRST:
             push(src, dst, step, q)
         turned.wait_send()
+    part = beam_part(blocks.at[0], wts, (0, 1), s, 0, LT)
+    beam[...] = part[:ROWS]
+    out_part[...] = part[ROWS:].astype(BF)
     build_windows(blocks.at[0], lens, left)
-    process(0)
+    vis_block(0, 0)
+    part_copy.start()
     for q in range(NCH):
-        for src, dst, step in second(q):
-            push(src, dst, step, q)
-    for slot in (4, 1, 3):
-        process(slot)
+        if q % 2 == 0:
+            push(3, 7, ACROSS, q)
+            push(4, 5, UP, q)
+        else:
+            push(1, 5, ACROSS, q)
+            push(4, 7, DOWN, q)
     for q in range(NCH):
-        push(*third(q), q)
-    for slot in (2, 5, 7):
-        process(slot)
-    process_last(6, LT - 1)
+        arrive(1 if q % 2 == 0 else 3, q)
+
+        sender = (y == 0) if q == 2 else ~middle if q % 2 == 0 else middle
+
+        @pl.when(sender)
+        def _():
+            if q % 2 == 0:
+                copy(1, 2, q, UP).start()
+            else:
+                copy(3, 2, q, DOWN).start()
+
+        if q == 2:
+            arrive(3, q)
+            pl.when(y == 1)(spare_copy.start)
+
+    def last_hop(q):
+        if q % 2 == 0:
+            arrive(5, q)
+
+            @pl.when(middle)
+            def _():
+                copy(5, 2, q, UP).start()
+        else:
+            arrive(7, q)
+
+            @pl.when(~middle)
+            def _():
+                copy(7, 2, q, DOWN).start()
+
+    process(4)
+    process(1)
+    last_hop(0)
+    last_hop(1)
+    process(3)
+    last_hop(2)
+    last_hop(3)
+    process(7)
+    process(5)
+    cut = LT - 1
+    late = (s + 2) % NS
+    arrive(2, *range(cut))
+    acc[...] = products(blocks.at[2], left, 0, cut)
+    part_copy.wait_recv()
+    beam[...] += in_part[...].astype(F32)
+    head = beam[:, : cut * 128] + beam_part(blocks.at[2], wts, (0,), late, 0, cut)
+    sums[...] = window_powers(head, lens, 0)
+    arrive(2, cut)
+    rest = beam[:, cut * 128 :] + beam_part(blocks.at[2], wts, (0,), late, cut, LT)
+    total = sums[...] + window_powers(rest, lens, cut)
+    for j in range(INTEG):
+        power[j] = total[j : j + 1] / jnp.full((1, SHARE), lens[j], jnp.int32).astype(F32)
+
+    def put(j, p, value):
+        vis[0, 2, j, 0, p] = value
+
+    average(acc[...] + products(blocks.at[2], left, cut, LT), lens, put)
     for cp in sends:
         cp.wait_send()
+    for q in range(NCH):
+        if q == 2:
+            pl.when(y < 3)(copy(0, 2, q, UP).wait_send)
+        else:
+            copy(0, 2, q, UP).wait_send()
+    pl.when(y == 1)(spare_copy.wait_send)
+    part_copy.wait_send()
 
 
 def store_kernel(vis_in, power_in, vis, power, sem):
@@ -331,17 +385,21 @@
             pltpu.VMEM((NC, 2, 4, SAMPLES), BF),
             pltpu.VMEM((LT, NC, 2, 4, 128), BF),
             pltpu.VMEM((NC, 8, 128), F32),
-            pltpu.VMEM((2, SHARE, NS * BLK), BF),
+            pltpu.VMEM((2, 2, SHARE, NS * BLK), BF),
             pltpu.VMEM((INTEG * BLK, 2 * SAMPLES), BF),
             pltpu.VMEM((2 * SHARE, SAMPLES), F32),
             pltpu.VMEM((INTEG * BLK, 2 * BLK), F32),
             pltpu.VMEM((8, SHARE), F32),
+            pltpu.VMEM((ROWS, SAMPLES), BF),
+            pltpu.VMEM((ROWS, SAMPLES), BF),
             pltpu.SemaphoreType.DMA((5,)),
             pltpu.SemaphoreType.DMA((NCH,)),
             pltpu.SemaphoreType.DMA((NCH,)),
             pltpu.SemaphoreType.DMA((NCH,)),
             pltpu.SemaphoreType.DMA((NS, NCH)),
             pltpu.SemaphoreType.DMA((NS, NCH)),
+            pltpu.SemaphoreType.DMA,
+            pltpu.SemaphoreType.DMA,
         ],
         compiler_params=pltpu.CompilerParams(
             collective_id=0, has_side_effects=True, vmem_limit_bytes=VMEM_LIMIT

time: 35.1 us -> 34.1 us (0.972)
  Pallas kernels: 34.4 us -> 33.3 us
    pallas_call x1, Pallas kernels: 33.3 us -> 32.2 us  [local(): pl.pallas_call(kernel, out_shape=(jax.ShapeDtypeStruct((1, OFFS, INTEG, 1...]
where the time goes in v4:
time: 34.1 us; the launch traced here: 33.9 us
  Pallas kernels  33.3 us (98%)
  between operations  0.64 us (2%)
    pallas_call x1, Pallas kernels, local(): pl.pallas_call(kernel, out_shape=(jax.ShapeDtypeStruct((1, OFFS, INTEG, 1...  32.2 us
    pallas_call x1, Pallas kernels, store(): pl.pallas_call(store_kernel, out_shape=(jax.ShapeDtypeStruct(vis.shape, v...  1.08 us

profile of v4, /device:TPU:1, one launch (start us, length us, event | category | flops | bytes accessed | tf_op | source)
XLA Modules:
  0.0 33.9 jit_solution(12392835863680605883)
XLA Ops:
  0.6 32.2 %correlator.1 = (bf16[1,5,4,1,2,128,128]{6,5,4,3,2,1,0:T(8,128)(2,1)S(1)}, f32[4,1,32]{2,1,0:T(1,128)S(1)}) custom-call(s32[4]{0:T(128)} %ph_hbm.1, s32[4]{0:T(128)} %lens_hbm.1, bf16[32,2,4,512]{3,2,1,0:T(4,128)(2,1)} %v_hbm.1, bf16[2,256,1024]{2,1,0:T(8,128)(2,1)} %w_hbm.1), custom_call_target="tpu_custom_call" | custom-call | tf_op jit(solution)/shard_map/correlator/pallas_call | solution.py:368
  32.9 1.1 %store.1 = (bf16[1,5,4,1,2,128,128]{6,5,4,3,2,1,0:T(8,128)(2,1)}, f32[4,1,32]{2,1,0:T(1,128)}) custom-call(bf16[1,5,4,1,2,128,128]{6,5,4,3,2,1,0:T(8,128)(2,1)S(1)} %get-tuple-element.4.vis_in, f32[4,1,32]{2,1,0:T(1,128)S(1)} %get-tuple-element.5.power_in), custom_call_target="tpu_custom_call" | custom-call | tf_op jit(solution)/shard_map/store/pallas_call | solution.py:353

commit v5 on v4

--- a/solution.py
+++ b/solution.py
@@ -243,6 +243,10 @@
         device_id={"chan": c, "stn": (s + 2) % NS}, device_id_type=MESH,
     )
 
+    fifth_copy = pltpu.make_async_remote_copy(
+        g.at[4, :, NCH - 1], g.at[5, :, NCH - 1], s2.at[6, 1], r2.at[5, NCH - 1],
+        device_id=to(UP), device_id_type=MESH,
+    )
     spare_copy = pltpu.make_async_remote_copy(
         g.at[3, :, 2], g.at[2, :, 2], s2.at[6, 0], r2.at[2, 2],
         device_id=to(DOWN), device_id_type=MESH,
@@ -268,8 +272,14 @@
             push(3, 7, ACROSS, q)
             push(4, 5, UP, q)
         else:
-            push(1, 5, ACROSS, q)
+            if q < NCH - 1:
+                push(1, 5, ACROSS, q)
+            else:
+                arrive(1, q)
+                pl.when(y < 2)(copy(1, 5, q, ACROSS).start)
             push(4, 7, DOWN, q)
+            if q == NCH - 1:
+                pl.when(middle)(fifth_copy.start)
     for q in range(NCH):
         arrive(1 if q % 2 == 0 else 3, q)
 
@@ -308,13 +318,22 @@
     last_hop(2)
     last_hop(3)
     process(7)
-    process(5)
+    q5, k5 = block_at(5)
+    arrive(5, 0, 1, 2)
+    beam[:, : 3 * 128] += beam_part(blocks.at[5], wts, (0,), q5, 0, 3)
+    arrive(5, 3)
+    beam[:, 3 * 128 :] += beam_part(blocks.at[5], wts, (0,), q5, 3, LT)
+
+    @pl.when(k5 < OFFS)
+    def _():
+        vis_block(5, k5)
+
+    part_copy.wait_recv()
+    beam[...] += in_part[...].astype(F32)
     cut = LT - 1
     late = (s + 2) % NS
     arrive(2, *range(cut))
     acc[...] = products(blocks.at[2], left, 0, cut)
-    part_copy.wait_recv()
-    beam[...] += in_part[...].astype(F32)
     head = beam[:, : cut * 128] + beam_part(blocks.at[2], wts, (0,), late, 0, cut)
     sums[...] = window_powers(head, lens, 0)
     arrive(2, cut)
@@ -335,6 +354,8 @@
         else:
             copy(0, 2, q, UP).wait_send()
     pl.when(y == 1)(spare_copy.wait_send)
+    pl.when(y < 2)(copy(1, 5, NCH - 1, ACROSS).wait_send)
+    pl.when(middle)(fifth_copy.wait_send)
     part_copy.wait_send()
 
 

time: 34.1 us -> 34 us (level)
  no operation moved by 1% of the time
where the time goes in v5:
time: 34 us; the launch traced here: 33.9 us
  Pallas kernels  33.3 us (98%)
  between operations  0.64 us (2%)
    pallas_call x1, Pallas kernels, local(): pl.pallas_call(kernel, out_shape=(jax.ShapeDtypeStruct((1, OFFS, INTEG, 1...  32.2 us
    pallas_call x1, Pallas kernels, store(): pl.pallas_call(store_kernel, out_shape=(jax.ShapeDtypeStruct(vis.shape, v...  1.08 us

profile of v5, /device:TPU:1, one launch (start us, length us, event | category | flops | bytes accessed | tf_op | source)
XLA Modules:
  0.0 33.9 jit_solution(11555642448587538770)
XLA Ops:
  0.6 32.2 %correlator.1 = (bf16[1,5,4,1,2,128,128]{6,5,4,3,2,1,0:T(8,128)(2,1)S(1)}, f32[4,1,32]{2,1,0:T(1,128)S(1)}) custom-call(s32[4]{0:T(128)} %ph_hbm.1, s32[4]{0:T(128)} %lens_hbm.1, bf16[32,2,4,512]{3,2,1,0:T(4,128)(2,1)} %v_hbm.1, bf16[2,256,1024]{2,1,0:T(8,128)(2,1)} %w_hbm.1), custom_call_target="tpu_custom_call" | custom-call | tf_op jit(solution)/shard_map/correlator/pallas_call | solution.py:389
  32.9 1.1 %store.1 = (bf16[1,5,4,1,2,128,128]{6,5,4,3,2,1,0:T(8,128)(2,1)}, f32[4,1,32]{2,1,0:T(1,128)}) custom-call(bf16[1,5,4,1,2,128,128]{6,5,4,3,2,1,0:T(8,128)(2,1)S(1)} %get-tuple-element.4.vis_in, f32[4,1,32]{2,1,0:T(1,128)S(1)} %get-tuple-element.5.power_in), custom_call_target="tpu_custom_call" | custom-call | tf_op jit(solution)/shard_map/store/pallas_call | solution.py:374

commit v6 on v5

--- a/solution.py
+++ b/solution.py
@@ -129,7 +129,7 @@
 
 
 UP, DOWN, ACROSS = (0, 1), (0, -1), (1, 0)
-FIRST = ((0, 4, ACROSS), (0, 1, UP), (0, 3, DOWN))
+FIRST = ((0, 1, UP), (0, 3, DOWN), (0, 4, ACROSS))
 ROWS = 2 * SHARE
 
 
@@ -146,7 +146,7 @@
 
     barrier = pltpu.get_barrier_semaphore()
 
-    for k in FAR:
+    for k in FAR[:8]:
         pl.semaphore_signal(
             barrier, 1, device_id={"chan": (c + k) % NC, "stn": s}, device_id_type=MESH
         )
@@ -155,6 +155,10 @@
     for k in (2, NS - 2):
         pl.semaphore_signal(
             barrier, 1, device_id={"chan": c, "stn": (s + k) % NS}, device_id_type=MESH
+        )
+    for k in FAR[8:]:
+        pl.semaphore_signal(
+            barrier, 1, device_id={"chan": (c + k) % NC, "stn": s}, device_id_type=MESH
         )
     load = pltpu.make_async_copy(v_hbm, vin, lsem.at[0])
     load.start()

time: 34 us -> 33.7 us (level)
  Pallas kernels: 33.3 us -> 32.7 us
    pallas_call x1, Pallas kernels: 32.2 us -> 31.6 us  [local(): pl.pallas_call(kernel, out_shape=(jax.ShapeDtypeStruct((1, OFFS, INTEG, 1...]
where the time goes in v6:
time: 33.7 us; the launch traced here: 33.3 us
  Pallas kernels  32.7 us (97%)
  between operations  0.64 us (2%)
    pallas_call x1, Pallas kernels, local(): pl.pallas_call(kernel, out_shape=(jax.ShapeDtypeStruct((1, OFFS, INTEG, 1...  31.6 us
    pallas_call x1, Pallas kernels, store(): pl.pallas_call(store_kernel, out_shape=(jax.ShapeDtypeStruct(vis.shape, v...  1.08 us

profile of v6, /device:TPU:1, one launch (start us, length us, event | category | flops | bytes accessed | tf_op | source)
XLA Modules:
  0.0 33.3 jit_solution(4013133545020710274)
XLA Ops:
  0.6 31.6 %correlator.1 = (bf16[1,5,4,1,2,128,128]{6,5,4,3,2,1,0:T(8,128)(2,1)S(1)}, f32[4,1,32]{2,1,0:T(1,128)S(1)}) custom-call(s32[4]{0:T(128)} %ph_hbm.1, s32[4]{0:T(128)} %lens_hbm.1, bf16[32,2,4,512]{3,2,1,0:T(4,128)(2,1)} %v_hbm.1, bf16[2,256,1024]{2,1,0:T(8,128)(2,1)} %w_hbm.1), custom_call_target="tpu_custom_call" | custom-call | tf_op jit(solution)/shard_map/correlator/pallas_call | solution.py:393
  32.3 1.1 %store.1 = (bf16[1,5,4,1,2,128,128]{6,5,4,3,2,1,0:T(8,128)(2,1)}, f32[4,1,32]{2,1,0:T(1,128)}) custom-call(bf16[1,5,4,1,2,128,128]{6,5,4,3,2,1,0:T(8,128)(2,1)S(1)} %get-tuple-element.4.vis_in, f32[4,1,32]{2,1,0:T(1,128)S(1)} %get-tuple-element.5.power_in), custom_call_target="tpu_custom_call" | custom-call | tf_op jit(solution)/shard_map/store/pallas_call | solution.py:378

commit v7 on v6

--- a/solution.py
+++ b/solution.py
@@ -146,17 +146,13 @@
 
     barrier = pltpu.get_barrier_semaphore()
 
-    for k in FAR[:8]:
-        pl.semaphore_signal(
-            barrier, 1, device_id={"chan": (c + k) % NC, "stn": s}, device_id_type=MESH
-        )
     for step in (UP, DOWN, ACROSS):
         pl.semaphore_signal(barrier, 1, device_id=to(step), device_id_type=MESH)
     for k in (2, NS - 2):
         pl.semaphore_signal(
             barrier, 1, device_id={"chan": c, "stn": (s + k) % NS}, device_id_type=MESH
         )
-    for k in FAR[8:]:
+    for k in FAR:
         pl.semaphore_signal(
             barrier, 1, device_id={"chan": (c + k) % NC, "stn": s}, device_id_type=MESH
         )

time: 33.7 us -> 33.8 us (level)
  Pallas kernels: 32.7 us -> 33.1 us
    pallas_call x1, Pallas kernels: 31.6 us -> 32 us  [local(): pl.pallas_call(kernel, out_shape=(jax.ShapeDtypeStruct((1, OFFS, INTEG, 1...]
where the time goes in v7:
time: 33.8 us; the launch traced here: 33.7 us
  Pallas kernels  33.1 us (98%)
  between operations  0.64 us (2%)
    pallas_call x1, Pallas kernels, local(): pl.pallas_call(kernel, out_shape=(jax.ShapeDtypeStruct((1, OFFS, INTEG, 1...  32 us
    pallas_call x1, Pallas kernels, store(): pl.pallas_call(store_kernel, out_shape=(jax.ShapeDtypeStruct(vis.shape, v...  1.08 us

profile of v7, /device:TPU:1, one launch (start us, length us, event | category | flops | bytes accessed | tf_op | source)
XLA Modules:
  0.0 33.7 jit_solution(14256671305171129895)
XLA Ops:
  0.6 32.0 %correlator.1 = (bf16[1,5,4,1,2,128,128]{6,5,4,3,2,1,0:T(8,128)(2,1)S(1)}, f32[4,1,32]{2,1,0:T(1,128)S(1)}) custom-call(s32[4]{0:T(128)} %ph_hbm.1, s32[4]{0:T(128)} %lens_hbm.1, bf16[32,2,4,512]{3,2,1,0:T(4,128)(2,1)} %v_hbm.1, bf16[2,256,1024]{2,1,0:T(8,128)(2,1)} %w_hbm.1), custom_call_target="tpu_custom_call" | custom-call | tf_op jit(solution)/shard_map/correlator/pallas_call | solution.py:389
  32.7 1.1 %store.1 = (bf16[1,5,4,1,2,128,128]{6,5,4,3,2,1,0:T(8,128)(2,1)}, f32[4,1,32]{2,1,0:T(1,128)}) custom-call(bf16[1,5,4,1,2,128,128]{6,5,4,3,2,1,0:T(8,128)(2,1)S(1)} %get-tuple-element.4.vis_in, f32[4,1,32]{2,1,0:T(1,128)S(1)} %get-tuple-element.5.power_in), custom_call_target="tpu_custom_call" | custom-call | tf_op jit(solution)/shard_map/store/pallas_call | solution.py:374
